TPU v7x, 32 devices: a whole 2x2x4 slice. The times are simulated.
32 devices in a mesh: parts: 1, tile: 16 (over z, y, core), face: 2 (over x), sub: 1.
Axes of the slice: x: 2, y: 2, z: 4, core: 2. Of those that a mesh axis runs over, the one named last changes fastest.
Arguments:
- fields: bfloat16 [96, 4, 32, 96], P('sub', 'face', 'tile', 'parts'), may hold values from -6 to 6
- upstream: bfloat16 [96, 4, 32, 96], P('sub', 'face', 'tile', 'parts'), may hold values from -6 to 6
- kernel_one: bfloat16 [3, 3, 96, 96], replicated, may hold values from -0.21875 to 0.21875
- kernel_two: bfloat16 [3, 3, 96, 96], replicated, may hold values from -0.21875 to 0.21875
Outputs:
- result: bfloat16 [96, 4, 32, 96], P('sub', 'face', 'tile', 'parts')
- fields_grad: bfloat16 [96, 4, 32, 96], P('sub', 'face', 'tile', 'parts')
- kernel_one_grad: float32 [3, 3, 96, 96], P('parts', None, None, 'sub')
- kernel_two_grad: float32 [3, 3, 96, 96], P('parts', None, None, 'sub')
All inputs are finite; a program needn't handle non-finite values.
Results may differ from a plain program's by a relative error of at most 0.0049.
Values may be sent and summed in bfloat16 or wider, within the bound.
A program may use at most 128 MiB of HBM per device.

v0:
```python
import jax
import jax.numpy as jnp
from jax import lax
from jax.sharding import PartitionSpec as P


def for_sending(x):

    def short(part):
        return part.astype(jnp.bfloat16) if part.dtype == jnp.float32 else part

    return jax.tree.map(short, x)


def extended(cells, sides, width):
    for axis, dim in sides:
        count = lax.axis_size(axis)
        head = lax.slice_in_dim(cells, 0, width, axis=dim)
        tail = lax.slice_in_dim(cells, cells.shape[dim] - width, cells.shape[dim], axis=dim)
        cells = jnp.concatenate(
            [
                lax.ppermute(tail, axis, [(i, (i + 1) % count) for i in range(count)]),
                cells,
                lax.ppermute(head, axis, [((i + 1) % count, i) for i in range(count)]),
            ],
            axis=dim,
        )
    return cells


def spread_2(block, axis, source):
    block = jnp.where(lax.axis_index(axis) == source, block, jnp.zeros_like(block))
    return lax.psum(block, axis)


def activate(values):
    return jax.nn.gelu(values, approximate=True)


def whole_channels(field):
    return jax.tree.map(
        lambda part, own: part.astype(own.dtype),
        lax.all_gather(for_sending(field), "sub", axis=0, tiled=True),
        field,
    )


def trade_edges(bundle):
    return extended(bundle, (("tile", 2), ("face", 1)), 1)


def copy_line(line_data, root):
    return jax.tree.map(lambda part: spread_2(part, "tile", root), line_data)


def collect_rows(pieces):
    return lax.all_gather(pieces, "tile", axis=3, tiled=True)


def select_table(tile_count, columns, offset, keep_all):
    width = columns + 2
    line_len = tile_count * columns
    source = lax.broadcasted_iota(jnp.int32, (tile_count * width, line_len), 0)
    target = lax.broadcasted_iota(jnp.int32, (tile_count * width, line_len), 1)
    place = source // width
    within = source % width
    hits = target == place * columns + within + offset
    if not keep_all:
        hits = jnp.logical_and(hits, within < columns)
    return jnp.where(hits, 1.0, 0.0).astype(jnp.float32)


def place_rows(flat_rows, table):
    return jnp.dot(
        flat_rows, table, precision=lax.Precision.HIGHEST, preferred_element_type=jnp.float32
    )


def sphere_pad_local(field):
    tile_count = lax.axis_size("tile")
    tile_place = lax.axis_index("tile")
    is_first = tile_place == 0
    is_last = tile_place == tile_count - 1
    channels, groups, columns, height = field.shape
    face_side = height // 3
    line_len = height + columns
    first_slot = jnp.concatenate([field[:, :, 0, :], field[:, :, :, 0]], axis=2)
    last_slot = jnp.concatenate([field[:, :, columns - 1, :], field[:, :, :, height - 1]], axis=2)
    got = trade_edges(jnp.stack([first_slot, last_slot], axis=2).astype(jnp.float32))
    prev_stack = got[:, 0:groups]
    own_cycle = got[:, 1 : groups + 1]
    next_stack = got[:, 2 : groups + 2]
    row_parts = jnp.stack(
        [prev_stack[:, :, 1, height:line_len], next_stack[:, :, 2, height:line_len]], axis=2
    )
    row_parts = jnp.pad(row_parts, ((0, 0), (0, 0), (0, 0), (0, 2)))
    gathered = collect_rows(row_parts)
    whole_rows = place_rows(gathered, select_table(tile_count, columns, 0, False))
    top_line = copy_line(next_stack[:, :, 1, 0:face_side], 0)
    bottom_line = copy_line(prev_stack[:, :, 2, 2 * face_side : height], tile_count - 1)
    edge_pad = ((0, 0), (0, 0), (1, 1))
    top_row = lax.dynamic_slice_in_dim(
        jnp.pad(top_line, edge_pad), tile_place * columns, columns + 2, 2
    )
    bottom_row = lax.dynamic_slice_in_dim(
        jnp.pad(bottom_line, edge_pad), tile_place * columns, columns + 2, 2
    )
    left_col = jnp.where(
        is_first,
        jnp.concatenate([whole_rows[:, :, 0], prev_stack[:, :, 0, 0 : 2 * face_side]], axis=2),
        own_cycle[:, :, 0, 0:height],
    )
    right_col = jnp.where(
        is_last,
        jnp.concatenate([next_stack[:, :, 3, face_side:height], whole_rows[:, :, 1]], axis=2),
        own_cycle[:, :, 3, 0:height],
    )
    middle = jnp.concatenate(
        [
            left_col.astype(jnp.bfloat16)[:, :, None],
            field,
            right_col.astype(jnp.bfloat16)[:, :, None],
        ],
        axis=2,
    )
    return jnp.concatenate(
        [
            top_row.astype(jnp.bfloat16)[..., None],
            middle,
            bottom_row.astype(jnp.bfloat16)[..., None],
        ],
        axis=3,
    )


def sphere_fold_local(gradient):
    tile_count = lax.axis_size("tile")
    tile_place = lax.axis_index("tile")
    is_first = tile_place == 0
    is_last = tile_place == tile_count - 1
    channels, groups, wide_cols, tall_rows = gradient.shape
    columns = wide_cols - 2
    height = tall_rows - 2
    face_side = height // 3
    line_len = height + columns
    interior = gradient[:, :, 1 : columns + 1, 1 : height + 1]
    grad_top = gradient[:, :, :, 0]
    grad_bottom = gradient[:, :, :, height + 1]
    grad_left = gradient[:, :, 0, 1 : height + 1]
    grad_right = gradient[:, :, columns + 1, 1 : height + 1]
    gathered = collect_rows(jnp.stack([grad_top, grad_bottom], axis=2))
    line_grads = place_rows(gathered, select_table(tile_count, columns, -1, True))
    prev_line = copy_line(grad_left[:, :, 0:face_side], 0)
    next_line = copy_line(grad_right[:, :, 2 * face_side : height], tile_count - 1)
    prev_piece = lax.dynamic_slice_in_dim(prev_line, tile_place * columns, columns, 2)
    next_piece = lax.dynamic_slice_in_dim(next_line, tile_place * columns, columns, 2)
    cycle = jnp.zeros((channels, groups + 2, 4, line_len), jnp.float32)
    cycle = cycle.at[:, 1 : groups + 1, 0, 0:height].add(jnp.where(is_first, 0.0, grad_left))
    cycle = cycle.at[:, 1 : groups + 1, 3, 0:height].add(jnp.where(is_last, 0.0, grad_right))
    cycle = cycle.at[:, 0:groups, 0, 0 : 2 * face_side].add(
        jnp.where(is_first, grad_left[:, :, face_side:height], 0.0)
    )
    cycle = cycle.at[:, 2 : groups + 2, 3, face_side:height].add(
        jnp.where(is_last, grad_right[:, :, 0 : 2 * face_side], 0.0)
    )
    cycle = cycle.at[:, 0:groups, 1, height:line_len].add(prev_piece)
    cycle = cycle.at[:, 2 : groups + 2, 2, height:line_len].add(next_piece)
    cycle = cycle.at[:, 2 : groups + 2, 1, 0:face_side].add(
        jnp.where(is_first, line_grads[:, :, 0], 0.0)
    )
    cycle = cycle.at[:, 0:groups, 2, 2 * face_side : height].add(
        jnp.where(is_last, line_grads[:, :, 1], 0.0)
    )
    returned = trade_edges(cycle)
    slot_sums = returned[:, :, 2:4] + jnp.concatenate(
        [returned[:, :, 0:1], returned[:, :, 5:6]], axis=2
    )
    edge_grads = (
        slot_sums[:, 2 : groups + 2]
        + jnp.pad(slot_sums[:, 0:1], ((0, 0), (0, groups - 1), (0, 0), (0, 0)))
        + jnp.pad(slot_sums[:, groups + 3 : groups + 4], ((0, 0), (groups - 1, 0), (0, 0), (0, 0)))
    )
    first_grad = edge_grads[:, :, 0]
    last_grad = edge_grads[:, :, 1]
    total = interior.at[:, :, 0, :].add(first_grad[:, :, 0:height])
    total = total.at[:, :, columns - 1, :].add(last_grad[:, :, 0:height])
    total = total.at[:, :, :, 0].add(first_grad[:, :, height:line_len])
    total = total.at[:, :, :, height - 1].add(last_grad[:, :, height:line_len])
    return total


def padded_input(field):
    return sphere_pad_local(whole_channels(field))


def convolve(padded, kernel):
    return lax.conv_general_dilated(
        padded,
        kernel,
        (1, 1),
        "VALID",
        dimension_numbers=("CNHW", "HWIO", "CNHW"),
        preferred_element_type=jnp.float32,
    )


def spread(cotangent, kernel):
    flipped = jnp.flip(kernel, (0, 1)).transpose(0, 1, 3, 2)
    return lax.conv_general_dilated(
        cotangent,
        flipped,
        (1, 1),
        ((2, 2), (2, 2)),
        dimension_numbers=("CNHW", "HWIO", "CNHW"),
        preferred_element_type=jnp.float32,
    )


def weight_terms(padded, cotangent):
    columns = cotangent.shape[2]
    height = cotangent.shape[3]
    flat_cot = cotangent.reshape(cotangent.shape[0], -1)
    tap_rows = []
    for col_tap in range(3):
        row_list = []
        for row_tap in range(3):
            tap_cells = padded[
                :, :, col_tap : col_tap + columns, row_tap : row_tap + height
            ].reshape(padded.shape[0], -1)
            row_list.append(
                lax.dot_general(
                    tap_cells,
                    flat_cot,
                    (((1,), (1,)), ((), ())),
                    preferred_element_type=jnp.float32,
                )
            )
        tap_rows.append(jnp.stack(row_list))
    return jnp.stack(tap_rows)


def on_device(fields, upstream, kernel_one, kernel_two):
    half_count = fields.shape[0]
    half_at = lax.axis_index("sub")
    face_side = fields.shape[2] * lax.axis_size("tile")
    cell_scale = 1.0 / (face_side * jnp.sqrt(jnp.float32(12.0)))
    out_one = lax.dynamic_slice_in_dim(kernel_one, half_at * half_count, half_count, 3)
    out_two = lax.dynamic_slice_in_dim(kernel_two, half_at * half_count, half_count, 3)
    in_one = lax.dynamic_slice_in_dim(kernel_one, half_at * half_count, half_count, 2)
    in_two = lax.dynamic_slice_in_dim(kernel_two, half_at * half_count, half_count, 2)
    padded_one = padded_input(fields)
    pre_one = convolve(padded_one, out_one)
    hidden = activate(pre_one).astype(jnp.bfloat16)
    padded_two = padded_input(hidden)
    result = convolve(padded_two, out_two).astype(jnp.bfloat16)
    hidden_grad = sphere_fold_local(spread(whole_channels(upstream), in_two))
    unused, pullback = jax.vjp(activate, pre_one)
    pre_grad = pullback(hidden_grad)[0].astype(jnp.bfloat16)
    fields_grad = sphere_fold_local(spread(whole_channels(pre_grad), in_one)).astype(jnp.bfloat16)
    kernel_one_grad = weight_terms(padded_one, pre_grad) * cell_scale
    kernel_two_grad = weight_terms(padded_two, upstream) * cell_scale
    kernel_one_grad, kernel_two_grad = lax.psum(
        (kernel_one_grad, kernel_two_grad), ("tile", "face")
    )
    return (result, fields_grad, kernel_one_grad, kernel_two_grad)


def solution(mesh):
    placed = (P("sub", "face", "tile", "parts"), P("sub", "face", "tile", "parts"), P(), P())
    return jax.shard_map(
        on_device,
        mesh=mesh,
        in_specs=placed,
        out_specs=(
            P("sub", "face", "tile", "parts"),
            P("sub", "face", "tile", "parts"),
            P("parts", None, None, "sub"),
            P("parts", None, None, "sub"),
        ),
        check_vma=False,
    )
```

profile of v0, /device:TPU:0, one launch (start us, length us, event | category | flops | bytes accessed | tf_op | source)
XLA Modules:
  0.0 541.0 jit_solution(8414374650207984221)
XLA Ops:
  10.8 1.2 copy.1063
  12.9 5.0 collective-permute-start.1
  19.3 1.6 convolution_select_fusion.1
  23.0 19.7 %all_gather.18 = f32[96,2,2,64]{0,2,1,3:T(2,128)S(1)} all-gather(f32[96,2,2,4]{0,2,1,3:T(2,128)S(1)} %copy.966), channel_id=1, replica_groups=mesh['parts'=1,'tile'=16,'face'=2,'sub'=1] {'tile'}, dimensions={3}, use_global_device_ids=true | all-gather | bytes 104448 | tf_op jit(solution)/shard_map/all_gather | solution.py:57
  44.3 1.6 collective-permute-start.2
  46.4 5.7 %collective-permute-done.2 = f32[96,1,4,98]{3,0,1,2:T(8,128)S(1)} collective-permute-done((f32[96,1,4,98]{3,0,1,2:T(8,128)S(1)}, f32[96,1,4,98]{3,0,1,2:T(8,128)S(1)}, u32[]{:S(2)}, u32[]{:S(2)}) %collective-permute-start.2) | collective-permute-done | bytes 150560 | tf_op jit(solution)/shard_map/ppermute | solution.py:24
  52.2 3.6 collective-permute-done.3
  55.9 62.0 %all-reduce.18 = (bf16[96,2,32]{2,0,1:T(8,128)(2,1)S(1)}, bf16[96,2,32]{2,0,1:T(8,128)(2,1)S(1)}, f32[96,2,32]{2,0,1:T(8,128)}, f32[96,2,32]{2,0,1:T(8,128)}) all-reduce(f32[96,2,32]{2,0,1:T(8,128)S(1)} %get-tuple-element.373, f32[96,2,32]{2,0,1:T(8,128)S(1)} %get-tuple-element.372, ...), channel_id=1, replica_groups=mesh['parts'=1,'tile'=16,'face'=2,'sub'=1] {'tile'}, use_global_device_ids=true, to_apply=%region_1.2 | all-reduce | flops 24576 | bytes 172032 | tf_op jit(solution)/shard_map/psum | solution.py:33
  117.9 1.5 copy.938
  119.4 1.5 copy.939
  122.8 17.5 %all_gather.16 = f32[96,2,2,64]{0,2,1,3:T(2,128)S(1)} all-gather(f32[96,2,2,4]{0,2,1,3:T(2,128)S(1)} %pad.117.clone), channel_id=1, replica_groups=mesh['parts'=1,'tile'=16,'face'=2,'sub'=1] {'tile'}, dimensions={3}, use_global_device_ids=true | all-gather | bytes 104448 | tf_op jit(solution)/shard_map/all_gather | solution.py:57
  141.8 1.4 subtract_multiply_fusion
  143.4 3.6 copy.1065
  149.5 15.8 %collective-permute-start.5 = (f32[96,2,1,98]{3,0,1,2:T(8,128)}, f32[96,2,1,98]{3,0,1,2:T(8,128)S(1)}, u32[]{:S(2)}, u32[]{:S(2)}) collective-permute-start(f32[96,2,1,98]{3,0,1,2:T(8,128)} %get-tuple-element.389), channel_id=1, source_target_pairs={{2,0},{4,2},{6,4},{8,6},{10,8},{12,10},{14,12},{16,14},{18,16},{20... | collective-permute-start | bytes 225800 | tf_op jit(solution)/shard_map/ppermute | solution.py:24
  170.1 4.4 collective-permute-start.9
  176.2 1.5 collective-permute-start.6
  180.8 6.0 %copy.1069 = f32[2,2,96,96]{0,3,1,2:T(8,128)} copy(f32[2,2,96,96]{3,0,2,1:T(2,128)} %slice.1337) | data formatting | bytes 294912
  188.5 5.9 %copy.1070 = f32[2,2,96,96]{0,3,1,2:T(8,128)} copy(f32[2,2,96,96]{3,0,2,1:T(2,128)} %slice.1338) | data formatting | bytes 294912
  196.2 5.9 %copy.1071 = f32[2,2,96,96]{0,3,1,2:T(8,128)} copy(f32[2,2,96,96]{3,0,2,1:T(2,128)} %slice.1339) | data formatting | bytes 294912
  203.9 6.0 %copy.1072 = f32[2,2,96,96]{0,3,1,2:T(8,128)} copy(f32[2,2,96,96]{3,0,2,1:T(2,128)} %slice.1340) | data formatting | bytes 294912
  210.7 1.5 collective-permute-start.10
  214.6 17.5 %all_gather.17 = f32[96,2,2,64]{0,2,1,3:T(2,128)S(1)} all-gather(f32[96,2,2,4]{0,2,1,3:T(2,128)S(1)} %pad.120.clone), channel_id=1, replica_groups=mesh['parts'=1,'tile'=16,'face'=2,'sub'=1] {'tile'}, dimensions={3}, use_global_device_ids=true | all-gather | bytes 104448 | tf_op jit(solution)/shard_map/all_gather | solution.py:57
  237.7 5.7 %copy.974 = f32[96,2,2,96]{2,0,1,3:T(8,128)} copy(f32[96,2,2,96]{3,0,1,2:T(8,128)S(1)} %fusion.95) | data formatting | bytes 294912 | tf_op jit(solution)/shard_map/scatter-add | solution.py:186
  243.4 1.2 copy.973
  245.4 1.6 fusion.91
  247.0 16.7 %fusion.2 = bf16[96,2,2,96]{2,0,1,3:T(8,128)(2,1)S(1)} fusion(f32[2,2,96,96]{0,3,1,2:T(8,128)} %copy.1072, f32[96,2,2,96]{2,0,1,3:T(8,128)} %fusion.91, f32[2,2,96,96]{0,3,1,2:T(8,128)} %copy.1069, f32[2,2,96,96]{0,3,1,2:T(8,128)} %copy.1071, f32[2,2,96,96]{0,3,1,2:T(8,128)} %copy.1070), kind=kLoop, calls=%fused_computation.4 | loop fusion | flops 368640 | bytes 811008 | tf_op jit(solution)/shard_map/convert_element_type | solution.py:258
  263.7 2.2 copy-done.1
  265.9 1.4 pad.132
  267.4 4.0 fusion.5
  271.5 5.2 copy.983
  278.1 63.9 %all-reduce.19 = (bf16[96,2,32]{2,0,1:T(8,128)(2,1)S(1)}, bf16[96,2,32]{2,0,1:T(8,128)(2,1)S(1)}, f32[96,2,32]{2,0,1:T(8,128)}, f32[96,2,32]{2,0,1:T(8,128)S(1)}) all-reduce(f32[96,2,32]{2,0,1:T(8,128)S(1)} %copy-done.8, f32[96,2,32]{2,0,1:T(8,128)S(1)} %copy-done.7, ...), channel_id=1, replica_groups=mesh['parts'=1,'tile'=16,'face'=2,'sub'=1] {'tile'}, use_global_device_ids=true, to_apply=%region_3.4 | all-reduce | flops 24576 | bytes 172032 | tf_op jit(solution)/shard_map/psum | solution.py:33
  342.0 1.5 copy.955
  343.6 1.5 copy.956
  350.2 5.5 %copy.995 = bf16[96,2,2,96]{3,0,2,1:T(8,128)(2,1)S(1)} copy(bf16[96,2,2,96]{2,0,1,3:T(8,128)(2,1)} %copy-done.1) | data formatting | bytes 147456 | tf_op jit(solution)/shard_map/convert_element_type | solution.py:258
  363.1 17.7 %all_gather.19 = f32[96,2,2,64]{0,2,1,3:T(2,128)S(1)} all-gather(f32[96,2,2,4]{0,2,1,3:T(2,128)S(1)} %copy.988), channel_id=1, replica_groups=mesh['parts'=1,'tile'=16,'face'=2,'sub'=1] {'tile'}, dimensions={3}, use_global_device_ids=true | all-gather | bytes 104448 | tf_op jit(solution)/shard_map/all_gather | solution.py:57
  386.6 4.1 collective-permute-start.13
  391.4 1.3 fusion.6
  398.9 1.6 collective-permute-start.14
  402.7 6.6 %collective-permute-done.14 = f32[96,1,6,98]{3,0,1,2:T(8,128)S(1)} collective-permute-done((f32[96,1,6,98]{3,0,1,2:T(8,128)S(1)}, f32[96,1,6,98]{3,0,1,2:T(8,128)S(1)}, u32[]{:S(2)}, u32[]{:S(2)}) %collective-permute-start.14) | collective-permute-done | bytes 225824 | tf_op jit(solution)/shard_map/ppermute | solution.py:22
  409.3 3.7 collective-permute-done.15
  413.5 5.7 %copy.993 = f32[96,2,2,96]{2,0,1,3:T(8,128)} copy(f32[96,2,2,96]{3,0,1,2:T(8,128)S(1)} %fusion.81) | data formatting | bytes 294912 | tf_op jit(solution)/shard_map/scatter-add | solution.py:186
  419.3 1.2 copy.992
  421.2 1.6 fusion.77
  422.9 7.1 %convert_element_type.73 = bf16[96,2,2,96]{2,0,1,3:T(8,128)(2,1)} convert(f32[96,2,2,96]{2,0,1,3:T(8,128)} %fusion.77) | non-fusion elementwise | flops 36864 | bytes 221184 | tf_op jit(solution)/shard_map/convert_element_type | solution.py:259
  430.0 6.2 %copy.1028 = bf16[96,2,2,96]{3,2,1,0:T(2,128)(2,1)} copy(bf16[96,2,2,96]{2,0,1,3:T(8,128)(2,1)} %convert_element_type.73) | data formatting | bytes 147456
  436.2 94.0 %all-reduce.17.cloned.1.call-done = (f32[3,3,96,96]{3,2,1,0:T(8,128)}, f32[3,3,96,96]{3,2,1,0:T(8,128)}) async-done(((f32[3,3,96,96]{3,2,1,0:T(8,128)}, f32[3,3,96,96]{3,2,1,0:T(8,128)}), (f32[3,3,96,96]{3,2,1,0:T(8,128)}, f32[3,3,96,96]{3,2,1,0:T(8,128)})) %all-reduce.17.cloned.1.call-update) | async-done | bytes 663568 | tf_op jit(solution)/shard_map/psum | solution.py:262
  530.2 1.8 copy.1164
  532.0 1.8 copy.1165
  (239 shorter events, 70.2 us)
Async XLA Ops:
  7.2 134.7 %copy-start = (bf16[3,3,96,96]{3,2,1,0:T(8,128)(2,1)S(1)}, bf16[3,3,96,96]{3,2,1,0:T(8,128)(2,1)}, u32[]{:S(2)}) copy-start(bf16[3,3,96,96]{3,2,1,0:T(8,128)(2,1)} %param.54) | copy-start | bytes 497668
  7.2 36.2 %copy-start.3 = (bf16[96,2,2,96]{3,2,1,0:T(2,128)(2,1)S(1)}, bf16[96,2,2,96]{3,2,1,0:T(2,128)(2,1)}, u32[]{:S(2)}) copy-start(bf16[96,2,2,96]{3,2,1,0:T(2,128)(2,1)} %param.52) | copy-start | bytes 221188
  7.2 523.0 %all-reduce.17.cloned.1.call-start = ((), (), s32[]{:S(2)}) async-start(), calls=%async_computation | async-start | bytes 1769472 | tf_op jit(solution)/shard_map/psum | solution.py:262
  12.3 31.9 %collective-permute-start = (f32[96,2,1,98]{3,0,1,2:T(8,128)S(1)}, f32[96,2,1,98]{3,0,1,2:T(8,128)S(1)}, u32[]{:S(2)}, u32[]{:S(2)}) collective-permute-start(f32[96,2,1,98]{3,0,1,2:T(8,128)S(1)} %get-tuple-element.390), channel_id=1, source_target_pairs={{0,2},{2,4},{4,6},{6,8},{8,10},{10,12},{12,14},{14,16},{16,18},{18... | collective-permute-start | bytes 225800 | tf_op jit(solution)/shard_map/ppermute | solution.py:22
  12.9 31.4 %collective-permute-start.1 = (f32[96,2,1,98]{3,0,1,2:T(8,128)S(1)}, f32[96,2,1,98]{3,0,1,2:T(8,128)S(1)}, u32[]{:S(2)}, u32[]{:S(2)}) collective-permute-start(f32[96,2,1,98]{3,0,1,2:T(8,128)S(1)} %get-tuple-element.391), channel_id=1, source_target_pairs={{2,0},{4,2},{6,4},{8,6},{10,8},{12,10},{14,12},{16,14},{18,16},{20... | collective-permute-start | bytes 225800 | tf_op jit(solution)/shard_map/ppermute | solution.py:24
  19.0 122.8 %copy-start.18 = (pred[16,13]{0,1:T(8,128)(4,1)S(1)}, pred[16,13]{0,1:T(8,128)(4,1)}, u32[]{:S(2)}) copy-start(pred[16,13]{0,1:T(8,128)(4,1)} %constant.743) | copy-start | bytes 628
  44.3 7.8 %collective-permute-start.2 = (f32[96,1,4,98]{3,0,1,2:T(8,128)S(1)}, f32[96,1,4,98]{3,0,1,2:T(8,128)S(1)}, u32[]{:S(2)}, u32[]{:S(2)}) collective-permute-start(f32[96,1,4,98]{3,0,1,2:T(8,128)S(1)} %get-tuple-element.374), channel_id=1, source_target_pairs={{1,0},{0,1},{3,2},{2,3},{5,4},{4,5},{7,6},{6,7},{9,8},{8,9},{11,10... | collective-permute-start | bytes 451592 | tf_op jit(solution)/shard_map/ppermute | solution.py:24
  45.9 9.9 %collective-permute-start.3 = (f32[96,1,4,98]{3,0,1,2:T(8,128)S(1)}, f32[96,1,4,98]{3,0,1,2:T(8,128)S(1)}, u32[]{:S(2)}, u32[]{:S(2)}) collective-permute-start(f32[96,1,4,98]{3,0,1,2:T(8,128)S(1)} %get-tuple-element.375), channel_id=1, source_target_pairs={{0,1},{1,0},{2,3},{3,2},{4,5},{5,4},{6,7},{7,6},{8,9},{9,8},{10,11... | collective-permute-start | bytes 451592 | tf_op jit(solution)/shard_map/ppermute | solution.py:22
  121.7 56.6 %copy-start.2 = (bf16[96,2,2,96]{3,2,1,0:T(2,128)(2,1)S(1)}, bf16[96,2,2,96]{3,2,1,0:T(2,128)(2,1)}, u32[]{:S(2)}) copy-start(bf16[96,2,2,96]{3,2,1,0:T(2,128)(2,1)} %param.53) | copy-start | bytes 221188
  140.9 26.3 %copy-start.14 = (f32[96,2,32]{2,0,1:T(8,128)S(1)}, f32[96,2,32]{2,0,1:T(8,128)}, u32[]{:S(2)}) copy-start(f32[96,2,32]{2,0,1:T(8,128)} %get-tuple-element.341) | copy-start | bytes 73732
  149.2 26.2 %collective-permute-start.4 = (f32[96,2,1,98]{3,0,1,2:T(8,128)}, f32[96,2,1,98]{3,0,1,2:T(8,128)S(1)}, u32[]{:S(2)}, u32[]{:S(2)}) collective-permute-start(f32[96,2,1,98]{3,0,1,2:T(8,128)} %get-tuple-element.388), channel_id=1, source_target_pairs={{0,2},{2,4},{4,6},{6,8},{8,10},{10,12},{12,14},{14,16},{16,18},{18... | collective-permute-start | bytes 225800 | tf_op jit(solution)/shard_map/ppermute | solution.py:22
  149.5 25.9 %collective-permute-start.5 = (f32[96,2,1,98]{3,0,1,2:T(8,128)}, f32[96,2,1,98]{3,0,1,2:T(8,128)S(1)}, u32[]{:S(2)}, u32[]{:S(2)}) collective-permute-start(f32[96,2,1,98]{3,0,1,2:T(8,128)} %get-tuple-element.389), channel_id=1, source_target_pairs={{2,0},{4,2},{6,4},{8,6},{10,8},{12,10},{14,12},{16,14},{18,16},{20... | collective-permute-start | bytes 225800 | tf_op jit(solution)/shard_map/ppermute | solution.py:24
  170.1 39.7 %collective-permute-start.8 = (f32[96,4,1,98]{3,0,1,2:T(8,128)}, f32[96,4,1,98]{3,0,1,2:T(8,128)S(1)}, u32[]{:S(2)}, u32[]{:S(2)}) collective-permute-start(f32[96,4,1,98]{3,0,1,2:T(8,128)} %get-tuple-element.350), channel_id=1, source_target_pairs={{0,2},{2,4},{4,6},{6,8},{8,10},{10,12},{12,14},{14,16},{16,18},{18... | collective-permute-start | bytes 451592 | tf_op jit(solution)/shard_map/ppermute | solution.py:22
  170.1 39.7 %collective-permute-start.9 = (f32[96,4,1,98]{3,0,1,2:T(8,128)}, f32[96,4,1,98]{3,0,1,2:T(8,128)S(1)}, u32[]{:S(2)}, u32[]{:S(2)}) collective-permute-start(f32[96,4,1,98]{3,0,1,2:T(8,128)} %get-tuple-element.351), channel_id=1, source_target_pairs={{2,0},{4,2},{6,4},{8,6},{10,8},{12,10},{14,12},{16,14},{18,16},{20... | collective-permute-start | bytes 451592 | tf_op jit(solution)/shard_map/ppermute | solution.py:24
  176.2 36.5 %collective-permute-start.6 = (f32[96,1,4,98]{3,0,1,2:T(8,128)}, f32[96,1,4,98]{3,0,1,2:T(8,128)S(1)}, u32[]{:S(2)}, u32[]{:S(2)}) collective-permute-start(f32[96,1,4,98]{3,0,1,2:T(8,128)} %get-tuple-element.368), channel_id=1, source_target_pairs={{1,0},{0,1},{3,2},{2,3},{5,4},{4,5},{7,6},{6,7},{9,8},{8,9},{11,10... | collective-permute-start | bytes 451592 | tf_op jit(solution)/shard_map/ppermute | solution.py:24
  177.7 35.0 %collective-permute-start.7 = (f32[96,1,4,98]{3,0,1,2:T(8,128)}, f32[96,1,4,98]{3,0,1,2:T(8,128)S(1)}, u32[]{:S(2)}, u32[]{:S(2)}) collective-permute-start(f32[96,1,4,98]{3,0,1,2:T(8,128)} %get-tuple-element.369), channel_id=1, source_target_pairs={{0,1},{1,0},{2,3},{3,2},{4,5},{5,4},{6,7},{7,6},{8,9},{9,8},{10,11... | collective-permute-start | bytes 451592 | tf_op jit(solution)/shard_map/ppermute | solution.py:22
  203.9 33.6 %copy-start.17 = (pred[2]{0:T(512)(128)(4,1)S(1)}, pred[2]{0:T(512)(128)(4,1)}, u32[]{:S(2)}) copy-start(pred[2]{0:T(512)(128)(4,1)} %constant.700.clone.1) | copy-start | bytes 10
  210.7 24.3 %collective-permute-start.10 = (f32[96,1,6,98]{3,0,1,2:T(8,128)}, f32[96,1,6,98]{3,0,1,2:T(8,128)}, u32[]{:S(2)}, u32[]{:S(2)}) collective-permute-start(f32[96,1,6,98]{3,0,1,2:T(8,128)} %get-tuple-element.346), channel_id=1, source_target_pairs={{0,1},{1,0},{2,3},{3,2},{4,5},{5,4},{6,7},{7,6},{8,9},{9,8},{10,11... | collective-permute-start | bytes 677384 | tf_op jit(solution)/shard_map/ppermute | solution.py:22
  212.2 22.8 %collective-permute-start.11 = (f32[96,1,6,98]{3,0,1,2:T(8,128)}, f32[96,1,6,98]{3,0,1,2:T(8,128)}, u32[]{:S(2)}, u32[]{:S(2)}) collective-permute-start(f32[96,1,6,98]{3,0,1,2:T(8,128)} %get-tuple-element.347), channel_id=1, source_target_pairs={{1,0},{0,1},{3,2},{2,3},{5,4},{4,5},{7,6},{6,7},{9,8},{8,9},{11,10... | collective-permute-start | bytes 677384 | tf_op jit(solution)/shard_map/ppermute | solution.py:24
  233.5 1.6 copy-start.5
  263.7 2.2 copy-start.1
  267.3 9.4 %copy-start.16 = (pred[16,13]{0,1:T(8,128)(4,1)S(1)}, pred[16,13]{0,1:T(8,128)(4,1)}, u32[]{:S(2)}) copy-start(pred[16,13]{0,1:T(8,128)(4,1)} %constant.745) | copy-start | bytes 628
  267.4 10.7 %copy-start.7 = (f32[96,2,32]{2,0,1:T(8,128)S(1)}, f32[96,2,32]{2,0,1:T(8,128)}, u32[]{:S(2)}) copy-start(f32[96,2,32]{2,0,1:T(8,128)} %get-tuple-element.366) | copy-start | bytes 73732
  267.4 10.7 %copy-start.8 = (f32[96,2,32]{2,0,1:T(8,128)S(1)}, f32[96,2,32]{2,0,1:T(8,128)}, u32[]{:S(2)}) copy-start(f32[96,2,32]{2,0,1:T(8,128)} %get-tuple-element.367) | copy-start | bytes 73732
  267.4 77.7 %copy-start.6 = (bf16[96,2,1,96]{3,0,2,1:T(8,128)(2,1)S(1)}, bf16[96,2,1,96]{3,0,2,1:T(8,128)(2,1)}, u32[]{:S(2)}) copy-start(bf16[96,2,1,96]{3,0,2,1:T(8,128)(2,1)} %copy-done.5) | copy-start | bytes 110596
  271.5 84.4 %copy-start.4 = (bf16[96,2,4,97]{3,0,2,1:T(8,128)(2,1)S(1)}, bf16[96,2,4,97]{3,0,2,1:T(8,128)(2,1)}, u32[]{:S(2)}) copy-start(bf16[96,2,4,97]{3,0,2,1:T(8,128)(2,1)} %get-tuple-element.383) | copy-start | bytes 446980
  349.4 33.7 %copy-start.15 = (f32[96,2,32]{2,0,1:T(8,128)S(1)}, f32[96,2,32]{2,0,1:T(8,128)}, u32[]{:S(2)}) copy-start(f32[96,2,32]{2,0,1:T(8,128)} %get-tuple-element.336) | copy-start | bytes 73732
  349.4 43.5 %copy-start.12 = (f32[1,96,96]{2,1,0:T(8,128)S(1)}, f32[1,96,96]{2,1,0:T(8,128)}, u32[]{:S(2)}) copy-start(f32[1,96,96]{2,1,0:T(8,128)} %convolution_bitcast_fusion.9) | copy-start | bytes 110596
  355.8 38.8 %copy-start.10 = (f32[1,96,96]{2,1,0:T(8,128)S(1)}, f32[1,96,96]{2,1,0:T(8,128)}, u32[]{:S(2)}) copy-start(f32[1,96,96]{2,1,0:T(8,128)} %convolution_bitcast_fusion.5) | copy-start | bytes 110596
  361.6 34.8 %copy-start.11 = (f32[1,96,96]{2,1,0:T(8,128)S(1)}, f32[1,96,96]{2,1,0:T(8,128)}, u32[]{:S(2)}) copy-start(f32[1,96,96]{2,1,0:T(8,128)} %convolution_bitcast_fusion.13) | copy-start | bytes 110596
  362.3 33.1 %copy-start.13 = (f32[1,96,96]{2,1,0:T(8,128)S(1)}, f32[1,96,96]{2,1,0:T(8,128)}, u32[]{:S(2)}) copy-start(f32[1,96,96]{2,1,0:T(8,128)} %convolution_bitcast_fusion.16) | copy-start | bytes 110596
  362.7 38.3 %copy-start.9 = (f32[1,96,96]{2,1,0:T(8,128)S(1)}, f32[1,96,96]{2,1,0:T(8,128)}, u32[]{:S(2)}) copy-start(f32[1,96,96]{2,1,0:T(8,128)} %convolution_bitcast_fusion.2) | copy-start | bytes 110596
  386.2 12.7 %collective-permute-start.12 = (f32[96,4,1,98]{3,0,1,2:T(8,128)S(1)}, f32[96,4,1,98]{3,0,1,2:T(8,128)S(1)}, u32[]{:S(2)}, u32[]{:S(2)}) collective-permute-start(f32[96,4,1,98]{3,0,1,2:T(8,128)S(1)} %get-tuple-element.348), channel_id=1, source_target_pairs={{0,2},{2,4},{4,6},{6,8},{8,10},{10,12},{12,14},{14,16},{16,18},{18... | collective-permute-start | bytes 451592 | tf_op jit(solution)/shard_map/ppermute | solution.py:22
  386.6 12.3 %collective-permute-start.13 = (f32[96,4,1,98]{3,0,1,2:T(8,128)S(1)}, f32[96,4,1,98]{3,0,1,2:T(8,128)S(1)}, u32[]{:S(2)}, u32[]{:S(2)}) collective-permute-start(f32[96,4,1,98]{3,0,1,2:T(8,128)S(1)} %get-tuple-element.349), channel_id=1, source_target_pairs={{2,0},{4,2},{6,4},{8,6},{10,8},{12,10},{14,12},{16,14},{18,16},{20... | collective-permute-start | bytes 451592 | tf_op jit(solution)/shard_map/ppermute | solution.py:24
  398.9 10.4 %collective-permute-start.14 = (f32[96,1,6,98]{3,0,1,2:T(8,128)S(1)}, f32[96,1,6,98]{3,0,1,2:T(8,128)S(1)}, u32[]{:S(2)}, u32[]{:S(2)}) collective-permute-start(f32[96,1,6,98]{3,0,1,2:T(8,128)S(1)} %get-tuple-element.344), channel_id=1, source_target_pairs={{0,1},{1,0},{2,3},{3,2},{4,5},{5,4},{6,7},{7,6},{8,9},{9,8},{10,11... | collective-permute-start | bytes 677384 | tf_op jit(solution)/shard_map/ppermute | solution.py:22
  400.5 12.6 %collective-permute-start.15 = (f32[96,1,6,98]{3,0,1,2:T(8,128)S(1)}, f32[96,1,6,98]{3,0,1,2:T(8,128)S(1)}, u32[]{:S(2)}, u32[]{:S(2)}) collective-permute-start(f32[96,1,6,98]{3,0,1,2:T(8,128)S(1)} %get-tuple-element.345), channel_id=1, source_target_pairs={{1,0},{0,1},{3,2},{2,3},{5,4},{4,5},{7,6},{6,7},{9,8},{8,9},{11,10... | collective-permute-start | bytes 677384 | tf_op jit(solution)/shard_map/ppermute | solution.py:24
Sparse Core Ops, SparseCore 0:
  402.8 127.3 all-reduce.16
where the time goes:
time: 551 us; the launch traced here: 541 us
  blocking collectives  198 us (36%)
  waiting for transfers between devices  114 us (21%)
  local copies, waits for them, and re-layouts  103 us (19%)
  other arithmetic  50.8 us (9%)
  starting transfers between devices  39 us (7%)
  matrix products  20.9 us (4%)
  between operations  15.6 us (3%)
    psum x2, blocking collectives, spread_2(): return lax.psum(block, axis)  126 us
    psum x1, waiting for transfers between devices, on_device(): lax.psum((kernel_one_grad, kernel_two_grad), ('tile', 'face'))  94 us
    all_gather x4, blocking collectives, collect_rows(): return lax.all_gather(pieces, 'tile', axis=3, tiled=True)  72.3 us
    unnamed x63, local copies, waits for them, and re-layouts  47 us
    ppermute x8, starting transfers between devices, extended(): lax.ppermute(head, axis, [((i + 1) % count, i) for i in range(count)])  33.5 us
    convert_element_type x1, other arithmetic, on_device(): pre_grad = pullback(hidden_grad)[0].astype(jnp.bfloat16)  16.7 us
    dot_general x18, matrix products, weight_terms(): lax.dot_general(tap_cells, flat_cot, (((1,), (1,)), ((), ())), preferred_...  13.9 us
    scatter-add x2, local copies, waits for them, and re-layouts, sphere_fold_local(): total = total.at[:, :, columns - 1, :].add(last_grad[:, :, 0:height])  11.4 us
  transfers between devices with their start and end apart: 17, of which 5 were waited for; matrix products, arithmetic and copies ran while one was open for 15% of the time, Pallas kernels for 0%

commit v1 on v0

--- a/solution.py
+++ b/solution.py
@@ -54,7 +54,7 @@
 
 
 def collect_rows(pieces):
-    return lax.all_gather(pieces, "tile", axis=3, tiled=True)
+    return jnp.concatenate(lax.all_gather(pieces, "tile"), axis=3)
 
 
 def select_table(tile_count, columns, offset, keep_all):

time: 551 us -> 651 us (1.18)
  blocking collectives: 198 us -> 284 us
  local copies, waits for them, and re-layouts: 103 us -> 122 us
  starting transfers between devices: 39 us -> 27.9 us
    all_gather x4, blocking collectives: 72.3 us -> 160 us  [collect_rows(): return jnp.concatenate(lax.all_gather(pieces, 'tile'), axis=3)]
    all_gather x0 -> x4, local copies, waits for them, and re-layouts: none -> 17 us  [collect_rows(): return jnp.concatenate(lax.all_gather(pieces, 'tile'), axis=3)]
    ppermute x8, starting transfers between devices: 33.5 us -> 22.4 us  [extended(): lax.ppermute(head, axis, [((i + 1) % count, i) for i in range(count)])]
    unnamed x63 -> x65, local copies, waits for them, and re-layouts: 47 us -> 46.1 us
where the time goes in v1:
time: 651 us; the launch traced here: 641 us
  blocking collectives  284 us (44%)
  local copies, waits for them, and re-layouts  122 us (19%)
  waiting for transfers between devices  114 us (18%)
  other arithmetic  54.4 us (8%)
  starting transfers between devices  27.9 us (4%)
  matrix products  23.3 us (4%)
  between operations  15.5 us (2%)
    all_gather x4, blocking collectives, collect_rows(): return jnp.concatenate(lax.all_gather(pieces, 'tile'), axis=3)  160 us
    psum x2, blocking collectives, spread_2(): return lax.psum(block, axis)  124 us
    psum x1, waiting for transfers between devices, on_device(): lax.psum((kernel_one_grad, kernel_two_grad), ('tile', 'face'))  95.6 us
    unnamed x65, local copies, waits for them, and re-layouts  46.1 us
    ppermute x8, starting transfers between devices, extended(): lax.ppermute(head, axis, [((i + 1) % count, i) for i in range(count)])  22.4 us
    all_gather x4, local copies, waits for them, and re-layouts, collect_rows(): return jnp.concatenate(lax.all_gather(pieces, 'tile'), axis=3)  17 us
    convert_element_type x1, other arithmetic, on_device(): pre_grad = pullback(hidden_grad)[0].astype(jnp.bfloat16)  16.7 us
    dot_general x18, matrix products, weight_terms(): lax.dot_general(tap_cells, flat_cot, (((1,), (1,)), ((), ())), preferred_...  14.5 us
  transfers between devices with their start and end apart: 17, of which 5 were waited for; matrix products, arithmetic and copies ran while one was open for 15% of the time, Pallas kernels for 0%

profile of v1, /device:TPU:0, one launch (start us, length us, event | category | flops | bytes accessed | tf_op | source)
XLA Modules:
  0.0 640.9 jit_solution(14214404803922552759)
XLA Ops:
  12.9 5.0 collective-permute-start.1
  19.3 1.6 convolution_select_fusion.1
  23.1 40.0 %all-gather.2 = f32[1536,2,2,4]{3,2,1,0:T(2,128)} all-gather(f32[96,2,2,4]{3,2,1,0:T(2,128)S(1)} %copy.853), channel_id=4, replica_groups=mesh['parts'=1,'tile'=16,'face'=2,'sub'=1] {'tile'}, dimensions={0}, use_global_device_ids=true | all-gather | bytes 104448 | tf_op jit(solution)/shard_map/all_gather | solution.py:57
  63.1 4.1 copy.854
  68.9 1.6 collective-permute-start.2
  71.0 5.7 collective-permute-done.2
  76.8 3.6 collective-permute-done.3
  80.5 62.0 %all-reduce.18 = (bf16[96,2,32]{2,0,1:T(8,128)(2,1)S(1)}, bf16[96,2,32]{2,0,1:T(8,128)(2,1)S(1)}, f32[96,2,32]{2,0,1:T(8,128)}, f32[96,2,32]{2,0,1:T(8,128)}) all-reduce(f32[96,2,32]{2,0,1:T(8,128)S(1)} %get-tuple-element.369, f32[96,2,32]{2,0,1:T(8,128)S(1)} %get-tuple-element.368, ...), channel_id=1, replica_groups=mesh['parts'=1,'tile'=16,'face'=2,'sub'=1] {'tile'}, use_global_device_ids=true, to_apply=%region_1.2 | all-reduce | flops 24576 | bytes 172032 | tf_op jit(solution)/shard_map/psum | solution.py:33
  142.5 1.5 copy.825
  144.0 1.5 copy.826
  145.9 41.0 %all-gather = f32[1536,2,2,4]{3,2,1,0:T(2,128)} all-gather(f32[96,2,2,4]{3,2,1,0:T(2,128)S(1)} %pad.117.clone), channel_id=2, replica_groups=mesh['parts'=1,'tile'=16,'face'=2,'sub'=1] {'tile'}, dimensions={0}, use_global_device_ids=true | all-gather | bytes 104448 | tf_op jit(solution)/shard_map/all_gather | solution.py:57
  186.9 4.1 copy.819
  194.1 3.6 copy.948
  200.3 4.5 collective-permute-start.5
  210.4 4.4 collective-permute-start.9
  216.6 1.5 collective-permute-start.6
  221.1 6.0 copy.952
  228.9 5.9 copy.953
  236.5 5.9 copy.954
  244.1 6.0 copy.955
  251.0 1.5 collective-permute-start.10
  253.4 39.0 %all-gather.1 = f32[1536,2,2,4]{3,2,1,0:T(2,128)} all-gather(f32[96,2,2,4]{3,2,1,0:T(2,128)S(1)} %pad.120.clone), channel_id=3, replica_groups=mesh['parts'=1,'tile'=16,'face'=2,'sub'=1] {'tile'}, dimensions={0}, use_global_device_ids=true | all-gather | bytes 104448 | tf_op jit(solution)/shard_map/all_gather | solution.py:57
  292.4 5.1 copy.836
  304.0 5.5 copy.861
  311.5 1.6 fusion.91
  313.1 16.7 %fusion.2 = bf16[96,2,2,96]{2,0,1,3:T(8,128)(2,1)S(1)} fusion(f32[2,2,96,96]{0,3,1,2:T(8,128)} %copy.955, f32[96,2,2,96]{2,0,1,3:T(8,128)} %fusion.91, f32[2,2,96,96]{0,3,1,2:T(8,128)} %copy.952, f32[2,2,96,96]{0,3,1,2:T(8,128)} %copy.954, f32[2,2,96,96]{0,3,1,2:T(8,128)} %copy.953), kind=kLoop, calls=%fused_computation.4 | loop fusion | flops 368640 | bytes 811008 | tf_op jit(solution)/shard_map/convert_element_type | solution.py:258
  329.8 2.2 copy-done.1
  332.0 1.4 pad.132
  333.6 4.0 fusion.5
  337.5 5.2 copy.870
  344.8 62.5 %all-reduce.19 = (bf16[96,2,32]{2,0,1:T(8,128)(2,1)S(1)}, bf16[96,2,32]{2,0,1:T(8,128)(2,1)S(1)}, f32[96,2,32]{2,0,1:T(8,128)}, f32[96,2,32]{2,0,1:T(8,128)}) all-reduce(f32[96,2,32]{2,0,1:T(8,128)S(1)} %copy-done.15, f32[96,2,32]{2,0,1:T(8,128)S(1)} %copy-done.14, ...), channel_id=1, replica_groups=mesh['parts'=1,'tile'=16,'face'=2,'sub'=1] {'tile'}, use_global_device_ids=true, to_apply=%region_3.4 | all-reduce | flops 24576 | bytes 172032 | tf_op jit(solution)/shard_map/psum | solution.py:33
  407.4 1.5 copy.842
  409.0 1.5 copy.843
  415.6 5.5 copy.882
  430.6 40.0 %all-gather.3 = f32[1536,2,2,4]{3,2,1,0:T(2,128)S(1)} all-gather(f32[96,2,2,4]{3,2,1,0:T(2,128)} %copy.875), channel_id=5, replica_groups=mesh['parts'=1,'tile'=16,'face'=2,'sub'=1] {'tile'}, dimensions={0}, use_global_device_ids=true | all-gather | bytes 104448 | tf_op jit(solution)/shard_map/all_gather | solution.py:57
  470.6 3.8 copy.876
  474.4 1.5 fusion.52
  485.5 4.3 collective-permute-start.13
  499.0 1.6 collective-permute-start.14
  502.8 4.8 collective-permute-done.14
  507.6 3.9 collective-permute-done.15
  512.1 5.7 copy.880
  519.7 1.6 fusion.77
  521.3 7.1 %convert_element_type.73 = bf16[96,2,2,96]{2,0,1,3:T(8,128)(2,1)} convert(f32[96,2,2,96]{2,0,1,3:T(8,128)} %fusion.77) | non-fusion elementwise | flops 36864 | bytes 221184 | tf_op jit(solution)/shard_map/convert_element_type | solution.py:259
  528.4 6.2 copy.915
  534.6 95.6 %all-reduce.17.cloned.1.call-done = (f32[3,3,96,96]{3,2,1,0:T(8,128)}, f32[3,3,96,96]{3,2,1,0:T(8,128)}) async-done(((f32[3,3,96,96]{3,2,1,0:T(8,128)}, f32[3,3,96,96]{3,2,1,0:T(8,128)}), (f32[3,3,96,96]{3,2,1,0:T(8,128)}, f32[3,3,96,96]{3,2,1,0:T(8,128)})) %all-reduce.17.cloned.1.call-update) | async-done | bytes 663568 | tf_op jit(solution)/shard_map/psum | solution.py:262
  630.2 1.8 copy.1047
  632.0 1.8 copy.1048
  (245 shorter events, 83.3 us)
Async XLA Ops:
  7.2 185.4 %copy-start = (bf16[3,3,96,96]{3,2,1,0:T(8,128)(2,1)S(1)}, bf16[3,3,96,96]{3,2,1,0:T(8,128)(2,1)}, u32[]{:S(2)}) copy-start(bf16[3,3,96,96]{3,2,1,0:T(8,128)(2,1)} %param.54) | copy-start | bytes 497668
  7.2 60.7 %copy-start.5 = (bf16[96,2,2,96]{3,2,1,0:T(2,128)(2,1)S(1)}, bf16[96,2,2,96]{3,2,1,0:T(2,128)(2,1)}, u32[]{:S(2)}) copy-start(bf16[96,2,2,96]{3,2,1,0:T(2,128)(2,1)} %param.52) | copy-start | bytes 221188
  7.2 623.0 %all-reduce.17.cloned.1.call-start = ((), (), s32[]{:S(2)}) async-start(), calls=%async_computation | async-start | bytes 1769472 | tf_op jit(solution)/shard_map/psum | solution.py:262
  12.3 56.5 %collective-permute-start = (f32[96,2,1,98]{3,0,1,2:T(8,128)S(1)}, f32[96,2,1,98]{3,0,1,2:T(8,128)S(1)}, u32[]{:S(2)}, u32[]{:S(2)}) collective-permute-start(f32[96,2,1,98]{3,0,1,2:T(8,128)S(1)} %get-tuple-element.386), channel_id=1, source_target_pairs={{0,2},{2,4},{4,6},{6,8},{8,10},{10,12},{12,14},{14,16},{16,18},{18... | collective-permute-start | bytes 225800 | tf_op jit(solution)/shard_map/ppermute | solution.py:22
  12.9 56.0 %collective-permute-start.1 = (f32[96,2,1,98]{3,0,1,2:T(8,128)S(1)}, f32[96,2,1,98]{3,0,1,2:T(8,128)S(1)}, u32[]{:S(2)}, u32[]{:S(2)}) collective-permute-start(f32[96,2,1,98]{3,0,1,2:T(8,128)S(1)} %get-tuple-element.387), channel_id=1, source_target_pairs={{2,0},{4,2},{6,4},{8,6},{10,8},{12,10},{14,12},{16,14},{18,16},{20... | collective-permute-start | bytes 225800 | tf_op jit(solution)/shard_map/ppermute | solution.py:24
  67.2 125.4 %copy-start.19 = (pred[16,13]{0,1:T(8,128)(4,1)S(1)}, pred[16,13]{0,1:T(8,128)(4,1)}, u32[]{:S(2)}) copy-start(pred[16,13]{0,1:T(8,128)(4,1)} %constant.743) | copy-start | bytes 628
  68.9 7.8 %collective-permute-start.2 = (f32[96,1,4,98]{3,0,1,2:T(8,128)S(1)}, f32[96,1,4,98]{3,0,1,2:T(8,128)S(1)}, u32[]{:S(2)}, u32[]{:S(2)}) collective-permute-start(f32[96,1,4,98]{3,0,1,2:T(8,128)S(1)} %get-tuple-element.370), channel_id=1, source_target_pairs={{1,0},{0,1},{3,2},{2,3},{5,4},{4,5},{7,6},{6,7},{9,8},{8,9},{11,10... | collective-permute-start | bytes 451592 | tf_op jit(solution)/shard_map/ppermute | solution.py:24
  70.5 9.9 %collective-permute-start.3 = (f32[96,1,4,98]{3,0,1,2:T(8,128)S(1)}, f32[96,1,4,98]{3,0,1,2:T(8,128)S(1)}, u32[]{:S(2)}, u32[]{:S(2)}) collective-permute-start(f32[96,1,4,98]{3,0,1,2:T(8,128)S(1)} %get-tuple-element.371), channel_id=1, source_target_pairs={{0,1},{1,0},{2,3},{3,2},{4,5},{5,4},{6,7},{7,6},{8,9},{9,8},{10,11... | collective-permute-start | bytes 451592 | tf_op jit(solution)/shard_map/ppermute | solution.py:22
  191.0 27.6 %copy-start.4 = (bf16[96,2,2,96]{3,2,1,0:T(2,128)(2,1)S(1)}, bf16[96,2,2,96]{3,2,1,0:T(2,128)(2,1)}, u32[]{:S(2)}) copy-start(bf16[96,2,2,96]{3,2,1,0:T(2,128)(2,1)} %param.53) | copy-start | bytes 221188
  191.6 35.5 %copy-start.8 = (bf16[96,2,1,96]{3,0,2,1:T(8,128)(2,1)}, bf16[96,2,1,96]{3,0,2,1:T(8,128)(2,1)S(1)}, u32[]{:S(2)}) copy-start(bf16[96,2,1,96]{3,0,2,1:T(8,128)(2,1)S(1)} %get-tuple-element.366) | copy-start | bytes 110596
  199.9 15.8 %collective-permute-start.4 = (f32[96,2,1,98]{3,0,1,2:T(8,128)}, f32[96,2,1,98]{3,0,1,2:T(8,128)S(1)}, u32[]{:S(2)}, u32[]{:S(2)}) collective-permute-start(f32[96,2,1,98]{3,0,1,2:T(8,128)} %get-tuple-element.384), channel_id=1, source_target_pairs={{0,2},{2,4},{4,6},{6,8},{8,10},{10,12},{12,14},{14,16},{16,18},{18... | collective-permute-start | bytes 225800 | tf_op jit(solution)/shard_map/ppermute | solution.py:22
  200.3 15.5 %collective-permute-start.5 = (f32[96,2,1,98]{3,0,1,2:T(8,128)}, f32[96,2,1,98]{3,0,1,2:T(8,128)S(1)}, u32[]{:S(2)}, u32[]{:S(2)}) collective-permute-start(f32[96,2,1,98]{3,0,1,2:T(8,128)} %get-tuple-element.385), channel_id=1, source_target_pairs={{2,0},{4,2},{6,4},{8,6},{10,8},{12,10},{14,12},{16,14},{18,16},{20... | collective-permute-start | bytes 225800 | tf_op jit(solution)/shard_map/ppermute | solution.py:24
  210.4 39.7 %collective-permute-start.8 = (f32[96,4,1,98]{3,0,1,2:T(8,128)}, f32[96,4,1,98]{3,0,1,2:T(8,128)S(1)}, u32[]{:S(2)}, u32[]{:S(2)}) collective-permute-start(f32[96,4,1,98]{3,0,1,2:T(8,128)} %get-tuple-element.346), channel_id=1, source_target_pairs={{0,2},{2,4},{4,6},{6,8},{8,10},{10,12},{12,14},{14,16},{16,18},{18... | collective-permute-start | bytes 451592 | tf_op jit(solution)/shard_map/ppermute | solution.py:22
  210.4 39.7 %collective-permute-start.9 = (f32[96,4,1,98]{3,0,1,2:T(8,128)}, f32[96,4,1,98]{3,0,1,2:T(8,128)S(1)}, u32[]{:S(2)}, u32[]{:S(2)}) collective-permute-start(f32[96,4,1,98]{3,0,1,2:T(8,128)} %get-tuple-element.347), channel_id=1, source_target_pairs={{2,0},{4,2},{6,4},{8,6},{10,8},{12,10},{14,12},{16,14},{18,16},{20... | collective-permute-start | bytes 451592 | tf_op jit(solution)/shard_map/ppermute | solution.py:24
  216.6 36.4 %collective-permute-start.6 = (f32[96,1,4,98]{3,0,1,2:T(8,128)}, f32[96,1,4,98]{3,0,1,2:T(8,128)S(1)}, u32[]{:S(2)}, u32[]{:S(2)}) collective-permute-start(f32[96,1,4,98]{3,0,1,2:T(8,128)} %get-tuple-element.364), channel_id=1, source_target_pairs={{1,0},{0,1},{3,2},{2,3},{5,4},{4,5},{7,6},{6,7},{9,8},{8,9},{11,10... | collective-permute-start | bytes 451592 | tf_op jit(solution)/shard_map/ppermute | solution.py:24
  218.1 34.9 %collective-permute-start.7 = (f32[96,1,4,98]{3,0,1,2:T(8,128)}, f32[96,1,4,98]{3,0,1,2:T(8,128)S(1)}, u32[]{:S(2)}, u32[]{:S(2)}) collective-permute-start(f32[96,1,4,98]{3,0,1,2:T(8,128)} %get-tuple-element.365), channel_id=1, source_target_pairs={{0,1},{1,0},{2,3},{3,2},{4,5},{5,4},{6,7},{7,6},{8,9},{9,8},{10,11... | collective-permute-start | bytes 451592 | tf_op jit(solution)/shard_map/ppermute | solution.py:22
  251.0 52.8 %copy-start.18 = (pred[2]{0:T(512)(128)(4,1)S(1)}, pred[2]{0:T(512)(128)(4,1)}, u32[]{:S(2)}) copy-start(pred[2]{0:T(512)(128)(4,1)} %constant.700.clone.1) | copy-start | bytes 10
  251.0 50.4 %collective-permute-start.10 = (f32[96,1,6,98]{3,0,1,2:T(8,128)}, f32[96,1,6,98]{3,0,1,2:T(8,128)}, u32[]{:S(2)}, u32[]{:S(2)}) collective-permute-start(f32[96,1,6,98]{3,0,1,2:T(8,128)} %get-tuple-element.342), channel_id=1, source_target_pairs={{0,1},{1,0},{2,3},{3,2},{4,5},{5,4},{6,7},{7,6},{8,9},{9,8},{10,11... | collective-permute-start | bytes 677384 | tf_op jit(solution)/shard_map/ppermute | solution.py:22
  252.5 48.9 %collective-permute-start.11 = (f32[96,1,6,98]{3,0,1,2:T(8,128)}, f32[96,1,6,98]{3,0,1,2:T(8,128)}, u32[]{:S(2)}, u32[]{:S(2)}) collective-permute-start(f32[96,1,6,98]{3,0,1,2:T(8,128)} %get-tuple-element.343), channel_id=1, source_target_pairs={{1,0},{0,1},{3,2},{2,3},{5,4},{4,5},{7,6},{6,7},{9,8},{8,9},{11,10... | collective-permute-start | bytes 677384 | tf_op jit(solution)/shard_map/ppermute | solution.py:24
  299.7 11.0 %copy-start.10 = (bf16[96,2,1,96]{3,0,2,1:T(8,128)(2,1)}, bf16[96,2,1,96]{3,0,2,1:T(8,128)(2,1)S(1)}, u32[]{:S(2)}) copy-start(bf16[96,2,1,96]{3,0,2,1:T(8,128)(2,1)S(1)} %get-tuple-element.354) | copy-start | bytes 110596
  299.7 11.0 %copy-start.12 = (bf16[96,2,1,96]{3,0,2,1:T(8,128)(2,1)}, bf16[96,2,1,96]{3,0,2,1:T(8,128)(2,1)S(1)}, u32[]{:S(2)}) copy-start(bf16[96,2,1,96]{3,0,2,1:T(8,128)(2,1)S(1)} %get-tuple-element.355) | copy-start | bytes 110596
  329.8 2.2 copy-start.1
  333.5 9.3 %copy-start.17 = (pred[16,13]{0,1:T(8,128)(4,1)S(1)}, pred[16,13]{0,1:T(8,128)(4,1)}, u32[]{:S(2)}) copy-start(pred[16,13]{0,1:T(8,128)(4,1)} %constant.745) | copy-start | bytes 628
  333.5 11.3 %copy-start.14 = (f32[96,2,32]{2,0,1:T(8,128)S(1)}, f32[96,2,32]{2,0,1:T(8,128)}, u32[]{:S(2)}) copy-start(f32[96,2,32]{2,0,1:T(8,128)} %get-tuple-element.362) | copy-start | bytes 73732
  333.5 11.3 %copy-start.15 = (f32[96,2,32]{2,0,1:T(8,128)S(1)}, f32[96,2,32]{2,0,1:T(8,128)}, u32[]{:S(2)}) copy-start(f32[96,2,32]{2,0,1:T(8,128)} %get-tuple-element.363) | copy-start | bytes 73732
  333.5 76.9 %copy-start.11 = (bf16[96,2,1,96]{3,0,2,1:T(8,128)(2,1)S(1)}, bf16[96,2,1,96]{3,0,2,1:T(8,128)(2,1)}, u32[]{:S(2)}) copy-start(bf16[96,2,1,96]{3,0,2,1:T(8,128)(2,1)} %copy-done.10) | copy-start | bytes 110596
  333.6 76.9 %copy-start.13 = (bf16[96,2,1,96]{3,0,2,1:T(8,128)(2,1)S(1)}, bf16[96,2,1,96]{3,0,2,1:T(8,128)(2,1)}, u32[]{:S(2)}) copy-start(bf16[96,2,1,96]{3,0,2,1:T(8,128)(2,1)} %copy-done.12) | copy-start | bytes 110596
  337.5 83.5 %copy-start.9 = (bf16[96,2,1,96]{3,0,2,1:T(8,128)(2,1)S(1)}, bf16[96,2,1,96]{3,0,2,1:T(8,128)(2,1)}, u32[]{:S(2)}) copy-start(bf16[96,2,1,96]{3,0,2,1:T(8,128)(2,1)} %copy-done.8) | copy-start | bytes 110596
  337.5 84.3 %copy-start.6 = (bf16[96,2,4,97]{3,0,2,1:T(8,128)(2,1)S(1)}, bf16[96,2,4,97]{3,0,2,1:T(8,128)(2,1)}, u32[]{:S(2)}) copy-start(bf16[96,2,4,97]{3,0,2,1:T(8,128)(2,1)} %get-tuple-element.379) | copy-start | bytes 446980
  343.9 85.9 %copy-start.2 = (f32[4,2,98,96]{2,3,1,0:T(8,128)}, f32[4,2,98,96]{2,3,1,0:T(8,128)S(1)}, u32[]{:S(2)}) copy-start(f32[4,2,98,96]{2,3,1,0:T(8,128)S(1)} %copy.956) | copy-start | bytes 903172
  344.7 64.3 %copy-start.7 = (f32[96,2,96]{2,0,1:T(8,128)}, f32[96,2,96]{2,0,1:T(8,128)S(1)}, u32[]{:S(2)}) copy-start(f32[96,2,96]{2,0,1:T(8,128)S(1)} %get-tuple-element.351) | copy-start | bytes 221188
  430.6 70.6 %copy-start.16 = (f32[1,96,96]{2,1,0:T(8,128)S(1)}, f32[1,96,96]{2,1,0:T(8,128)}, u32[]{:S(2)}) copy-start(f32[1,96,96]{2,1,0:T(8,128)} %convolution_bitcast_fusion.2) | copy-start | bytes 110596
  474.3 22.9 %copy-start.3 = (f32[4,2,98,96]{2,3,1,0:T(8,128)S(1)}, f32[4,2,98,96]{2,3,1,0:T(8,128)}, u32[]{:S(2)}) copy-start(f32[4,2,98,96]{2,3,1,0:T(8,128)} %copy-done.2) | copy-start | bytes 903172
  485.1 13.9 %collective-permute-start.12 = (f32[96,4,1,98]{3,0,1,2:T(8,128)S(1)}, f32[96,4,1,98]{3,0,1,2:T(8,128)S(1)}, u32[]{:S(2)}, u32[]{:S(2)}) collective-permute-start(f32[96,4,1,98]{3,0,1,2:T(8,128)S(1)} %get-tuple-element.344), channel_id=1, source_target_pairs={{0,2},{2,4},{4,6},{6,8},{8,10},{10,12},{12,14},{14,16},{16,18},{18... | collective-permute-start | bytes 451592 | tf_op jit(solution)/shard_map/ppermute | solution.py:22
  485.5 13.4 %collective-permute-start.13 = (f32[96,4,1,98]{3,0,1,2:T(8,128)S(1)}, f32[96,4,1,98]{3,0,1,2:T(8,128)S(1)}, u32[]{:S(2)}, u32[]{:S(2)}) collective-permute-start(f32[96,4,1,98]{3,0,1,2:T(8,128)S(1)} %get-tuple-element.345), channel_id=1, source_target_pairs={{2,0},{4,2},{6,4},{8,6},{10,8},{12,10},{14,12},{16,14},{18,16},{20... | collective-permute-start | bytes 451592 | tf_op jit(solution)/shard_map/ppermute | solution.py:24
  499.0 8.6 %collective-permute-start.14 = (f32[96,1,6,98]{3,0,1,2:T(8,128)S(1)}, f32[96,1,6,98]{3,0,1,2:T(8,128)S(1)}, u32[]{:S(2)}, u32[]{:S(2)}) collective-permute-start(f32[96,1,6,98]{3,0,1,2:T(8,128)S(1)} %get-tuple-element.340), channel_id=1, source_target_pairs={{0,1},{1,0},{2,3},{3,2},{4,5},{5,4},{6,7},{7,6},{8,9},{9,8},{10,11... | collective-permute-start | bytes 677384 | tf_op jit(solution)/shard_map/ppermute | solution.py:22
  500.6 11.0 %collective-permute-start.15 = (f32[96,1,6,98]{3,0,1,2:T(8,128)S(1)}, f32[96,1,6,98]{3,0,1,2:T(8,128)S(1)}, u32[]{:S(2)}, u32[]{:S(2)}) collective-permute-start(f32[96,1,6,98]{3,0,1,2:T(8,128)S(1)} %get-tuple-element.341), channel_id=1, source_target_pairs={{1,0},{0,1},{3,2},{2,3},{5,4},{4,5},{7,6},{6,7},{9,8},{8,9},{11,10... | collective-permute-start | bytes 677384 | tf_op jit(solution)/shard_map/ppermute | solution.py:24
Sparse Core Ops, SparseCore 0:
  502.9 127.2 all-reduce.16
